TPU v7x, 256 devices: a whole 4x4x8 slice. The times are simulated.
256 devices in a mesh: grp: 32 (over x, y, core), blk: 8 (over z).
Axes of the slice: x: 4, y: 4, z: 8, core: 2. Of those that a mesh axis runs over, the one named last changes fastest.
Arguments:
- tiles_near: bfloat16 [16384, 256, 256], P(('grp', 'blk')), may hold values from -0.078125 to 0.078125
- near_cols: int32 [256, 64], P(('grp', 'blk')), may hold values from 0 to 3
- tiles_far: bfloat16 [6144, 256, 256], P(('grp', 'blk')), may hold values from -0.078125 to 0.078125
- far_groups: int32 [256, 24], P(('grp', 'blk')), may hold values from 0 to 31, as said below
- need_blocks: int32 [256, 32], P(('grp', 'blk')), may hold values from -1 to 3, as said below
- start_vectors: bfloat16 [262144, 128], P(('grp', 'blk')), may hold values from -6 to 6
Outputs:
- vectors: float32 [262144, 128], P(('grp', 'blk'))
Inputs may be any that keep to these rules, and one draw needn't show every extreme that they name: need_blocks[d, h] is -1 for d's own group and for groups d reads nothing from, else a row block index below 4 of the device of group h at d's position along blk; every device reads from at least one other group. far_groups[d, t] is a group h with need_blocks[d, h] >= 0.
All inputs are finite; a program needn't handle non-finite values.
Results may differ from a plain program's by a relative error of at most 0.0029.
Values may be sent and summed in bfloat16 or wider, within the bound.
A program may use at most 128 MiB of HBM per device.

v0:
```python
import jax
import jax.numpy as jnp
from jax import lax
from jax.sharding import PartitionSpec as P

ITERS = 2


def per_device(tiles_near, near_cols, tiles_far, far_groups, need_blocks, start_vectors):
    tile_size = tiles_near.shape[1]
    vec_width = start_vectors.shape[1]
    blocks = start_vectors.shape[0] // tile_size
    group_size = lax.axis_size("blk")
    group_count = lax.axis_size("grp")
    per_source = tiles_near.shape[0] // (blocks * group_size)
    far_each = tiles_far.shape[0] // blocks
    near_tiles = tiles_near.reshape(blocks, group_size, per_source, tile_size, tile_size)
    near_index = near_cols.reshape(blocks, group_size, per_source)
    far_tiles = tiles_far.reshape(blocks, far_each, tile_size, tile_size)
    far_index = far_groups.reshape(blocks, far_each)
    wanted = need_blocks.reshape(group_count)
    total_rows = blocks * tile_size * group_size * group_count
    current = start_vectors
    vectors = start_vectors.astype(jnp.float32)
    for iteration in range(ITERS):
        local_rows = current.reshape(blocks, tile_size, vec_width)
        group_table = lax.all_gather(local_rows, "blk", axis=0, tiled=True)
        source_ids = jnp.arange(group_size, dtype=jnp.int32)[None, :, None]
        chosen = group_table[source_ids * blocks + near_index]
        near_part = jnp.einsum(
            "rmnij,rmnjk->rik", near_tiles, chosen, preferred_element_type=jnp.float32
        )
        everything = lax.all_gather(local_rows, "grp", axis=0, tiled=True)
        far_rows = everything[far_index * blocks + wanted[far_index]]
        far_part = jnp.einsum(
            "rnij,rnjk->rik", far_tiles, far_rows, preferred_element_type=jnp.float32
        )
        product = near_part + far_part
        flat_rows = product.reshape(blocks * tile_size, vec_width)
        local_gram = jnp.dot(
            flat_rows.T,
            flat_rows,
            precision=lax.Precision.HIGHEST,
            preferred_element_type=jnp.float32,
        )
        gram = lax.psum(local_gram, ("grp", "blk")) / total_rows
        factor = jnp.linalg.cholesky(gram)
        identity_matrix = jnp.eye(vec_width, dtype=jnp.float32)
        inverse = lax.linalg.triangular_solve(factor, identity_matrix, left_side=True, lower=True).T
        vectors = jnp.dot(
            flat_rows, inverse, precision=lax.Precision.HIGHEST, preferred_element_type=jnp.float32
        )
        current = vectors.astype(jnp.bfloat16)
    return vectors


def solution(mesh):
    in_specs = (
        P(("grp", "blk"), None, None),
        P(("grp", "blk"), None),
        P(("grp", "blk"), None, None),
        P(("grp", "blk"), None),
        P(("grp", "blk"), None),
        P(("grp", "blk"), None),
    )
    out_specs = P(("grp", "blk"), None)
    return jax.shard_map(
        per_device, mesh=mesh, in_specs=in_specs, out_specs=out_specs, check_vma=False
    )
```

profile of v0, /device:TPU:1, one launch (start us, length us, event | category | flops | bytes accessed | tf_op | source)
XLA Modules:
  0.0 777.3 jit_solution(7489281376360508679)
XLA Ops:
  6.5 0.7 all-gather.5.cloned.1.call-update
  7.3 0.7 all-gather.7.cloned.1.call-update
  8.1 0.5 broadcast.166
  8.6 1.3 reduce.10
  10.1 1.4 gather_fusion.1
  11.6 1.3 reduce.11
  12.9 0.1 reshape.117
  13.1 0.1 reshape.129
  13.3 37.1 %all-gather.5.cloned.1.call-done = bf16[32,256,128]{2,1,0:T(8,128)(2,1)} async-done(((bf16[4,256,128]{2,1,0:T(8,128)(2,1)}), bf16[32,256,128]{2,1,0:T(8,128)(2,1)}) %all-gather.5.cloned.1.call-update) | async-done | bytes 2097168 | tf_op jit(solution)/shard_map/all_gather | solution.py:27
  50.4 4.6 gather_fusion
  55.0 58.5 %all-gather.7.cloned.1.call-done = bf16[128,256,128]{2,1,0:T(8,128)(2,1)} async-done(((bf16[4,256,128]{2,1,0:T(8,128)(2,1)}), bf16[128,256,128]{2,1,0:T(8,128)(2,1)}) %all-gather.7.cloned.1.call-update) | async-done | bytes 8388624 | tf_op jit(solution)/shard_map/all_gather | solution.py:33
  113.6 5.4 gather_fusion.2
  118.9 2.7 convolution_bitcast_fusion.1
  121.7 5.2 fusion.31
  126.9 0.8 copy-done.1
  127.7 1.2 convolution_bitcast_fusion.3
  129.0 2.0 copy.32
  131.0 235.3 %all-reduce.3.cloned.1.call-done = f32[128,128]{0,1:T(8,128)} async-done(((f32[128,128]{0,1:T(8,128)}), f32[128,128]{0,1:T(8,128)}) %all-reduce.3.cloned.1.call-update) | async-done | bytes 65552 | tf_op jit(solution)/shard_map/psum | solution.py:46
  366.3 0.8 broadcast_multiply_fusion.1
  367.2 0.1 copy.35
  367.3 0.9 fusion.45
  368.1 11.7 %cholesky.44 = f32[128,128]{1,0:T(8,128)S(1)} custom-call(f32[128,128]{1,0:T(8,128)S(1)} %fusion.45), custom_call_target="Cholesky" | custom-call | tf_op jit(solution)/shard_map/jit(cholesky)/cholesky | solution.py:47
  379.9 0.6 compare_reduce_fusion.1
  380.5 0.7 fusion.40
  381.2 9.8 %custom-call.6 = f32[1,128,128]{1,2,0:T(8,128)S(1)} custom-call(f32[1,128,128]{2,1,0:T(8,128)S(1)} %fusion.40), custom_call_target="InvertDiagBlocksLowerTriangular" | custom-call | tf_op jit(solution)/shard_map/triangular_solve/custom-call.0 | solution.py:49
  391.0 0.3 fusion.38
  391.3 2.3 convolution_convert_fusion
  393.7 0.5 all-gather.11.cloned.1.call-update
  394.2 0.2 all-reduce.5.cloned.1.call-start
  394.5 32.8 %all-gather.9.cloned.1.call-done = bf16[32,256,128]{2,1,0:T(8,128)(2,1)} async-done(((bf16[4,256,128]{2,1,0:T(8,128)(2,1)}), bf16[32,256,128]{2,1,0:T(8,128)(2,1)}) %all-gather.9.cloned.1.call-update) | async-done | bytes 2097168 | tf_op jit(solution)/shard_map/all_gather | solution.py:27
  427.3 4.6 gather_fusion.3
  432.0 58.4 %all-gather.11.cloned.1.call-done = bf16[128,256,128]{2,1,0:T(8,128)(2,1)} async-done(((bf16[4,256,128]{2,1,0:T(8,128)(2,1)}), bf16[128,256,128]{2,1,0:T(8,128)(2,1)}) %all-gather.11.cloned.1.call-update) | async-done | bytes 8388624 | tf_op jit(solution)/shard_map/all_gather | solution.py:33
  490.3 5.4 gather_fusion.4
  495.7 2.7 convolution_bitcast_fusion
  498.4 5.2 fusion.21
  503.7 0.8 copy-done.2
  504.5 1.2 convolution_bitcast_fusion.2
  505.7 2.0 copy.39
  507.7 235.3 %all-reduce.5.cloned.1.call-done = f32[128,128]{0,1:T(8,128)} async-done(((f32[128,128]{0,1:T(8,128)}), f32[128,128]{0,1:T(8,128)}) %all-reduce.5.cloned.1.call-update) | async-done | bytes 65552 | tf_op jit(solution)/shard_map/psum | solution.py:46
  743.1 0.8 broadcast_multiply_fusion
  743.9 0.1 copy.42
  744.0 0.9 fusion.43
  744.9 11.7 %cholesky.55 = f32[128,128]{1,0:T(8,128)S(1)} custom-call(f32[128,128]{1,0:T(8,128)S(1)} %fusion.43), custom_call_target="Cholesky" | custom-call | tf_op jit(solution)/shard_map/jit(cholesky)/cholesky | solution.py:47
  756.6 0.6 compare_reduce_fusion
  757.2 0.7 fusion.41
  757.9 9.8 %custom-call.7 = f32[1,128,128]{1,2,0:T(8,128)S(1)} custom-call(f32[1,128,128]{2,1,0:T(8,128)S(1)} %fusion.41), custom_call_target="InvertDiagBlocksLowerTriangular" | custom-call | tf_op jit(solution)/shard_map/triangular_solve/custom-call.0 | solution.py:49
  767.7 0.3 fusion.36
  768.0 2.4 fusion.46
  (29 shorter events, 0.8 us)
Async XLA Ops:
  6.5 112.4 %copy-start = (bf16[24,256,256]{2,1,0:T(8,128)(2,1)S(1)}, bf16[24,256,256]{2,1,0:T(8,128)(2,1)}, u32[]{:S(2)}) copy-start(bf16[24,256,256]{2,1,0:T(8,128)(2,1)} %param.11) | copy-start | bytes 9437188
  6.5 43.8 %all-gather.5.cloned.1.call-start = ((), (), s32[]{:S(2)}) async-start(), calls=%async_computation | async-start | bytes 2359296 | tf_op jit(solution)/shard_map/all_gather | solution.py:27
  7.3 106.3 %all-gather.7.cloned.1.call-start = ((), (), s32[]{:S(2)}) async-start(), calls=%async_computation.1 | async-start | bytes 8650752 | tf_op jit(solution)/shard_map/all_gather | solution.py:33
  8.0 358.3 %all-reduce.3.cloned.1.call-start = ((), (), s32[]{:S(2)}) async-start(), calls=%async_computation.2 | async-start | bytes 131072 | tf_op jit(solution)/shard_map/psum | solution.py:46
  118.9 2.7 copy-start.4
  126.9 0.8 copy-start.1
  128.9 298.4 %all-gather.9.cloned.1.call-start = ((), (), s32[]{:S(2)}) async-start(), calls=%async_computation.3 | async-start | bytes 2359296 | tf_op jit(solution)/shard_map/all_gather | solution.py:27
  393.6 96.7 %all-gather.11.cloned.1.call-start = ((), (), s32[]{:S(2)}) async-start(), calls=%async_computation.4 | async-start | bytes 8650752 | tf_op jit(solution)/shard_map/all_gather | solution.py:33
  394.2 348.8 %all-reduce.5.cloned.1.call-start = ((), (), s32[]{:S(2)}) async-start(), calls=%async_computation.5 | async-start | bytes 131072 | tf_op jit(solution)/shard_map/psum | solution.py:46
  495.7 2.7 copy-start.3
  503.7 0.8 copy-start.2
Sparse Core Ops, SparseCore 0:
  9.1 41.1 all-gather.4
  52.9 60.5 all-gather.6
  129.1 237.2 all-reduce.2
  393.8 33.4 all-gather.8
  429.7 60.5 all-gather.10
  505.8 237.1 all-reduce.4
where the time goes:
time: 778 us; the launch traced here: 777 us
  waiting for transfers between devices  659 us (85%)
  other arithmetic  51.9 us (7%)
  local copies, waits for them, and re-layouts  28.3 us (4%)
  matrix products  23.6 us (3%)
  between operations  13.7 us (2%)
    psum x2, waiting for transfers between devices, per_device(): gram = lax.psum(local_gram, ('grp', 'blk')) / total_rows  471 us
    all_gather x2, waiting for transfers between devices, per_device(): everything = lax.all_gather(local_rows, 'grp', axis=0, tiled=True)  117 us
    all_gather x2, waiting for transfers between devices, per_device(): group_table = lax.all_gather(local_rows, 'blk', axis=0, tiled=True)  70 us
    another operation x6, other arithmetic, per_device(): factor = jnp.linalg.cholesky(gram)  24.8 us
    another operation x4, other arithmetic, per_device(): lax.linalg.triangular_solve(factor, identity_matrix, left_side=True, lowe...  20.9 us
  transfers between devices with their start and end apart: 6, of which 6 were waited for; matrix products, arithmetic and copies ran while one was open for 2% of the time, Pallas kernels for 0%

commit v1 on v0

--- a/solution.py
+++ b/solution.py
@@ -43,7 +43,12 @@
             precision=lax.Precision.HIGHEST,
             preferred_element_type=jnp.float32,
         )
-        gram = lax.psum(local_gram, ("grp", "blk")) / total_rows
+
+        def streams_put(incoming_x):
+            arr_now = jax.lax.psum(incoming_x, axis_name="blk")
+            return jax.lax.psum(arr_now, axis_name="grp")
+
+        gram = streams_put(local_gram) / total_rows
         factor = jnp.linalg.cholesky(gram)
         identity_matrix = jnp.eye(vec_width, dtype=jnp.float32)
         inverse = lax.linalg.triangular_solve(factor, identity_matrix, left_side=True, lower=True).T

time: 778 us -> 663 us (0.85)
  waiting for transfers between devices: 659 us -> 545 us
    psum x2 -> x4, waiting for transfers between devices: 471 us -> 353 us  [the longest x2 222 us: streams_put(): return jax.lax.psum(arr_now, axis_name='grp')]
  transfers between devices with their start and end apart: 6 -> 8, of which waited for: 6 -> 8; matrix products, arithmetic and copies ran while one was open for 2% -> 3% of each run, Pallas kernels for 0% -> 0%
where the time goes in v1:
time: 663 us
  waiting for transfers between devices  545 us (82%)
  other arithmetic  51.9 us (8%)
  local copies, waits for them, and re-layouts  28.3 us (4%)
  matrix products  23.6 us (4%)
  between operations  13.7 us (2%)
    psum x2, waiting for transfers between devices, streams_put(): return jax.lax.psum(arr_now, axis_name='grp')  222 us
    psum x2, waiting for transfers between devices, streams_put(): arr_now = jax.lax.psum(incoming_x, axis_name='blk')  132 us
    all_gather x2, waiting for transfers between devices, per_device(): everything = lax.all_gather(local_rows, 'grp', axis=0, tiled=True)  117 us
    all_gather x2, waiting for transfers between devices, per_device(): group_table = lax.all_gather(local_rows, 'blk', axis=0, tiled=True)  72.5 us
    another operation x6, other arithmetic, per_device(): factor = jnp.linalg.cholesky(gram)  24.8 us
    another operation x4, other arithmetic, per_device(): lax.linalg.triangular_solve(factor, identity_matrix, left_side=True, lowe...  20.9 us
  transfers between devices with their start and end apart: 8, of which 8 were waited for; matrix products, arithmetic and copies ran while one was open for 3% of the time, Pallas kernels for 0%

profile of v1, /device:TPU:1, one launch (start us, length us, event | category | flops | bytes accessed | tf_op | source)
XLA Modules:
  0.0 662.7 jit_solution(17956715218961829974)
XLA Ops:
  6.5 0.7 all-gather.5.cloned.1.call-update
  7.3 0.7 all-gather.7.cloned.1.call-update
  8.1 0.5 broadcast.166
  8.6 1.3 reduce.10
  10.1 1.4 gather_fusion.1
  11.6 1.3 reduce.11
  12.9 0.1 reshape.117
  13.1 0.1 reshape.129
  13.3 37.1 %all-gather.5.cloned.1.call-done = bf16[32,256,128]{2,1,0:T(8,128)(2,1)} async-done(((bf16[4,256,128]{2,1,0:T(8,128)(2,1)}), bf16[32,256,128]{2,1,0:T(8,128)(2,1)}) %all-gather.5.cloned.1.call-update) | async-done | bytes 2097168 | tf_op jit(solution)/shard_map/all_gather | solution.py:27
  50.4 4.6 gather_fusion
  55.0 58.5 %all-gather.7.cloned.1.call-done = bf16[128,256,128]{2,1,0:T(8,128)(2,1)} async-done(((bf16[4,256,128]{2,1,0:T(8,128)(2,1)}), bf16[128,256,128]{2,1,0:T(8,128)(2,1)}) %all-gather.7.cloned.1.call-update) | async-done | bytes 8388624 | tf_op jit(solution)/shard_map/all_gather | solution.py:33
  113.6 5.4 gather_fusion.2
  118.9 2.7 convolution_bitcast_fusion.1
  121.7 5.2 fusion.31
  126.9 0.8 copy-done.1
  127.7 1.2 convolution_bitcast_fusion.3
  129.0 65.8 %all-reduce.5.cloned.1.call-done = f32[128,128]{0,1:T(8,128)} async-done(((f32[128,128]{0,1:T(8,128)}), f32[128,128]{0,1:T(8,128)}) %all-reduce.5.cloned.1.call-update) | async-done | bytes 65552 | tf_op jit(solution)/shard_map/psum | solution.py:48
  194.9 2.0 copy.32
  196.9 110.8 %all-reduce.7.cloned.1.call-done = f32[128,128]{0,1:T(8,128)} async-done(((f32[128,128]{0,1:T(8,128)}), f32[128,128]{0,1:T(8,128)}) %all-reduce.7.cloned.1.call-update) | async-done | bytes 65552 | tf_op jit(solution)/shard_map/psum | solution.py:49
  307.7 0.8 broadcast_multiply_fusion.1
  308.6 0.9 fusion.45
  309.5 11.7 %cholesky.44 = f32[128,128]{1,0:T(8,128)S(1)} custom-call(f32[128,128]{1,0:T(8,128)S(1)} %fusion.45), custom_call_target="Cholesky" | custom-call | tf_op jit(solution)/shard_map/jit(cholesky)/cholesky | solution.py:52
  321.2 0.6 compare_reduce_fusion.1
  321.9 0.7 fusion.40
  322.5 9.8 %custom-call.6 = f32[1,128,128]{1,2,0:T(8,128)S(1)} custom-call(f32[1,128,128]{2,1,0:T(8,128)S(1)} %fusion.40), custom_call_target="InvertDiagBlocksLowerTriangular" | custom-call | tf_op jit(solution)/shard_map/triangular_solve/custom-call.0 | solution.py:54
  332.3 0.3 fusion.38
  332.6 2.3 convolution_convert_fusion
  335.0 0.5 all-gather.11.cloned.1.call-update
  335.6 0.2 all-reduce.9.cloned.1.call-start
  335.8 35.4 %all-gather.9.cloned.1.call-done = bf16[32,256,128]{2,1,0:T(8,128)(2,1)} async-done(((bf16[4,256,128]{2,1,0:T(8,128)(2,1)}), bf16[32,256,128]{2,1,0:T(8,128)(2,1)}) %all-gather.9.cloned.1.call-update) | async-done | bytes 2097168 | tf_op jit(solution)/shard_map/all_gather | solution.py:27
  371.2 4.6 gather_fusion.3
  375.9 58.4 %all-gather.11.cloned.1.call-done = bf16[128,256,128]{2,1,0:T(8,128)(2,1)} async-done(((bf16[4,256,128]{2,1,0:T(8,128)(2,1)}), bf16[128,256,128]{2,1,0:T(8,128)(2,1)}) %all-gather.11.cloned.1.call-update) | async-done | bytes 8388624 | tf_op jit(solution)/shard_map/all_gather | solution.py:33
  434.2 5.4 gather_fusion.4
  439.6 2.7 convolution_bitcast_fusion
  442.4 5.2 fusion.21
  447.6 0.8 copy-done.2
  448.4 1.2 convolution_bitcast_fusion.2
  449.7 65.8 %all-reduce.9.cloned.1.call-done = f32[128,128]{0,1:T(8,128)} async-done(((f32[128,128]{0,1:T(8,128)}), f32[128,128]{0,1:T(8,128)}) %all-reduce.9.cloned.1.call-update) | async-done | bytes 65552 | tf_op jit(solution)/shard_map/psum | solution.py:48
  515.5 2.0 copy.39
  517.5 110.9 %all-reduce.11.cloned.1.call-done = f32[128,128]{0,1:T(8,128)} async-done(((f32[128,128]{0,1:T(8,128)}), f32[128,128]{0,1:T(8,128)}) %all-reduce.11.cloned.1.call-update) | async-done | bytes 65552 | tf_op jit(solution)/shard_map/psum | solution.py:49
  628.5 0.8 broadcast_multiply_fusion
  629.4 0.9 fusion.43
  630.3 11.7 %cholesky.55 = f32[128,128]{1,0:T(8,128)S(1)} custom-call(f32[128,128]{1,0:T(8,128)S(1)} %fusion.43), custom_call_target="Cholesky" | custom-call | tf_op jit(solution)/shard_map/jit(cholesky)/cholesky | solution.py:52
  642.0 0.6 compare_reduce_fusion
  642.7 0.7 fusion.41
  643.3 9.8 %custom-call.7 = f32[1,128,128]{1,2,0:T(8,128)S(1)} custom-call(f32[1,128,128]{2,1,0:T(8,128)S(1)} %fusion.41), custom_call_target="InvertDiagBlocksLowerTriangular" | custom-call | tf_op jit(solution)/shard_map/triangular_solve/custom-call.0 | solution.py:54
  653.1 0.3 fusion.36
  653.4 2.4 fusion.46
  (35 shorter events, 1.0 us)
Async XLA Ops:
  6.5 112.4 %copy-start = (bf16[24,256,256]{2,1,0:T(8,128)(2,1)S(1)}, bf16[24,256,256]{2,1,0:T(8,128)(2,1)}, u32[]{:S(2)}) copy-start(bf16[24,256,256]{2,1,0:T(8,128)(2,1)} %param.11) | copy-start | bytes 9437188
  6.5 43.8 %all-gather.5.cloned.1.call-start = ((), (), s32[]{:S(2)}) async-start(), calls=%async_computation | async-start | bytes 2359296 | tf_op jit(solution)/shard_map/all_gather | solution.py:27
  7.3 106.3 %all-gather.7.cloned.1.call-start = ((), (), s32[]{:S(2)}) async-start(), calls=%async_computation.1 | async-start | bytes 8650752 | tf_op jit(solution)/shard_map/all_gather | solution.py:33
  8.0 186.8 %all-reduce.5.cloned.1.call-start = ((), (), s32[]{:S(2)}) async-start(), calls=%async_computation.2 | async-start | bytes 131072 | tf_op jit(solution)/shard_map/psum | solution.py:48
  118.9 2.7 copy-start.4
  126.9 0.8 copy-start.1
  128.9 178.7 %all-reduce.7.cloned.1.call-start = ((), (), s32[]{:S(2)}) async-start(), calls=%async_computation.3 | async-start | bytes 131072 | tf_op jit(solution)/shard_map/psum | solution.py:49
  194.8 176.4 %all-gather.9.cloned.1.call-start = ((), (), s32[]{:S(2)}) async-start(), calls=%async_computation.4 | async-start | bytes 2359296 | tf_op jit(solution)/shard_map/all_gather | solution.py:27
  335.0 99.3 %all-gather.11.cloned.1.call-start = ((), (), s32[]{:S(2)}) async-start(), calls=%async_computation.5 | async-start | bytes 8650752 | tf_op jit(solution)/shard_map/all_gather | solution.py:33
  335.6 179.9 %all-reduce.9.cloned.1.call-start = ((), (), s32[]{:S(2)}) async-start(), calls=%async_computation.6 | async-start | bytes 131072 | tf_op jit(solution)/shard_map/psum | solution.py:48
  439.6 2.7 copy-start.3
  447.6 0.8 copy-start.2
  449.6 178.9 %all-reduce.11.cloned.1.call-start = ((), (), s32[]{:S(2)}) async-start(), calls=%async_computation.7 | async-start | bytes 131072 | tf_op jit(solution)/shard_map/psum | solution.py:49
Sparse Core Ops, SparseCore 0:
  9.1 41.1 all-gather.4
  52.9 60.5 all-gather.6
  129.1 65.6 all-reduce.4
  198.3 109.3 all-reduce.6
  335.1 36.0 all-gather.8
  373.6 60.5 all-gather.10
  449.7 65.6 all-reduce.8
  519.1 109.3 all-reduce.10
